TPU v7x, 128 devices: a whole 4x4x4 slice. The times are simulated.
128 devices in a mesh: expert: 4 (over z), seq: 4 (over y), tensor: 8 (over x, core).
Axes of the slice: x: 4, y: 4, z: 4, core: 2. Of those that a mesh axis runs over, the one named last changes fastest.
Arguments:
- tokens: bfloat16 [3072, 7168], P(('expert', 'seq')), may hold values from -6 to 6
- grad_out: bfloat16 [3072, 7168], P(('expert', 'seq')), may hold values from -6 to 6
- expert_ids: int32 [3072, 2], P(('expert', 'seq')), may hold values from 0 to 3, all different within a row; in each aligned block of 192 rows (0 to 191, 192 to 383, ...) at most 128 rows name the same one
- route_weights: bfloat16 [3072, 2], P(('expert', 'seq')), may hold values from 0.099609375 to 1
- gate_weight: bfloat16 [4, 7168, 2048], P('expert', 'seq', 'tensor'), may hold values from -0.0625 to 0.0625
- up_weight: bfloat16 [4, 7168, 2048], P('expert', 'seq', 'tensor'), may hold values from -0.0625 to 0.0625
- down_weight: bfloat16 [4, 7168, 2048], P('expert', 'seq', 'tensor'), may hold values from -0.125 to 0.125
Outputs:
- grad_tokens: bfloat16 [3072, 7168], P(('expert', 'seq'), 'tensor')
- grad_route: float32 [3072, 2], P(('expert', 'seq'))
- grad_gate: float32 [4, 7168, 2048], P('expert', 'seq', 'tensor')
- grad_up: float32 [4, 7168, 2048], P('expert', 'seq', 'tensor')
- grad_down: float32 [4, 7168, 2048], P('expert', 'seq', 'tensor')
Inputs may be any that keep to these rules, and one draw needn't show every extreme that they name: `expert_ids`: the two ids of a row differ. Within each aligned block of 192 rows (the tokens of one group of the expert and seq axes) no expert is named by more than 128 rows, and in some block an expert is named by exactly 128 rows.
All inputs are finite; a program needn't handle non-finite values.
Results may differ from a plain program's by a relative error of at most 0.019.
Values may be sent and summed in bfloat16 or wider, within the bound.
A program may use at most 192 MiB of HBM per device.

v0:
```python
import jax
import jax.numpy as jnp
from jax import lax
from jax.sharding import PartitionSpec as P


def shards(tokens, grad_out, expert_ids, route_weights, gate_weight, up_weight, down_weight):
    expert_count = lax.axis_size("expert")
    seq_count = lax.axis_size("seq")
    tensor_count = lax.axis_size("tensor")
    local_count = gate_weight.shape[0]
    tok_rows = tokens.shape[0]
    model_width = tokens.shape[1]
    part_width = model_width // tensor_count
    per_peer = tok_rows // 6
    peer_count = expert_count * seq_count
    block_rows = local_count * per_peer
    slot_count = peer_count * block_rows
    flat_ids = expert_ids.reshape(-1)
    route_count = flat_ids.shape[0]
    onehot = (
        flat_ids[:, None] == jnp.arange(local_count * expert_count, dtype=jnp.int32)[None, :]
    ).astype(jnp.int32)
    before = jnp.cumsum(onehot, axis=0) - onehot
    ranking = jnp.sum(before * onehot, axis=1)
    local_expert = flat_ids % local_count
    dest_peer = flat_ids // local_count * seq_count + ranking % seq_count
    target = (dest_peer * local_count + local_expert) * per_peer + ranking // seq_count
    source = (
        jnp.full((slot_count,), -1, jnp.int32)
        .at[target]
        .set(jnp.arange(route_count, dtype=jnp.int32))
    )
    filled = source >= 0
    safe_source = jnp.maximum(source, 0)
    token_of = safe_source // 2
    keep = filled[:, None].astype(tokens.dtype)
    weight_send = (
        route_weights.reshape(-1)[safe_source] * filled.astype(route_weights.dtype)
    ).reshape(peer_count, block_rows)
    in_send = (tokens[token_of] * keep).reshape(peer_count, block_rows, model_width)
    out_send = (grad_out[token_of] * keep).reshape(peer_count, block_rows, model_width)
    in_recv, out_recv, weight_recv = (
        lax.all_to_all(in_send, ("expert", "seq"), split_axis=0, concat_axis=0, tiled=True),
        lax.all_to_all(out_send, ("expert", "seq"), split_axis=0, concat_axis=0, tiled=True),
        lax.all_to_all(weight_send, ("expert", "seq"), split_axis=0, concat_axis=0, tiled=True),
    )

    def by_expert(values):
        shaped = values.reshape((peer_count, local_count, per_peer) + values.shape[2:])
        return jnp.swapaxes(shaped, 0, 1).reshape(
            (local_count, peer_count * per_peer) + values.shape[2:]
        )

    def by_peer(values):
        shaped = values.reshape((local_count, peer_count, per_peer) + values.shape[2:])
        return jnp.swapaxes(shaped, 0, 1).reshape((peer_count, block_rows) + values.shape[2:])

    in_rows = by_expert(in_recv)
    out_rows = by_expert(out_recv)
    prob = by_expert(weight_recv).astype(jnp.float32)[:, :, None]
    gate_full, up_full, down_full = (
        lax.all_gather(gate_weight, "seq", axis=1, tiled=True),
        lax.all_gather(up_weight, "seq", axis=1, tiled=True),
        lax.all_gather(down_weight, "seq", axis=1, tiled=True),
    )
    pre_gate = jnp.einsum("emd,edf->emf", in_rows, gate_full, preferred_element_type=jnp.float32)
    pre_up = jnp.einsum("emd,edf->emf", in_rows, up_full, preferred_element_type=jnp.float32)
    sigmoid_gate = jax.nn.sigmoid(pre_gate)
    silu_gate = pre_gate * sigmoid_gate
    hidden = silu_gate * pre_up
    hidden_low = hidden.astype(jnp.bfloat16)
    back_proj = jnp.einsum("emd,edf->emf", out_rows, down_full, preferred_element_type=jnp.float32)
    partial_scores = jnp.sum(hidden * back_proj, axis=2)
    scaled = (prob * out_rows.astype(jnp.float32)).astype(jnp.bfloat16)
    hidden_grad = prob * back_proj
    up_grad = (hidden_grad * silu_gate).astype(jnp.bfloat16)
    gate_grad = (
        hidden_grad * pre_up * sigmoid_gate * (1.0 + pre_gate * (1.0 - sigmoid_gate))
    ).astype(jnp.bfloat16)
    input_terms = jnp.einsum(
        "emf,edf->emd", gate_grad, gate_full, preferred_element_type=jnp.float32
    )
    input_terms = input_terms + jnp.einsum(
        "emf,edf->emd", up_grad, up_full, preferred_element_type=jnp.float32
    )
    route_scores = lax.psum(partial_scores, "tensor")
    input_shards = lax.psum_scatter(
        input_terms.astype(jnp.bfloat16), "tensor", scatter_dimension=2, tiled=True
    ).astype(jnp.float32)
    back_rows, back_scores = (
        lax.all_to_all(
            by_peer(input_shards).astype(jnp.bfloat16),
            ("expert", "seq"),
            split_axis=0,
            concat_axis=0,
            tiled=True,
        ).astype(jnp.float32),
        lax.all_to_all(
            by_peer(route_scores).astype(jnp.bfloat16),
            ("expert", "seq"),
            split_axis=0,
            concat_axis=0,
            tiled=True,
        ).astype(jnp.float32),
    )
    route_rows = back_rows.reshape(slot_count, part_width)[target].reshape(tok_rows, 2, part_width)
    grad_tokens = jnp.sum(route_rows, axis=1).astype(jnp.bfloat16)
    grad_route = back_scores.reshape(slot_count)[target].reshape(tok_rows, 2)
    gate_part = jnp.einsum("emd,emf->edf", in_rows, gate_grad, preferred_element_type=jnp.float32)
    up_part = jnp.einsum("emd,emf->edf", in_rows, up_grad, preferred_element_type=jnp.float32)
    down_part = jnp.einsum("emd,emf->edf", scaled, hidden_low, preferred_element_type=jnp.float32)
    grad_gate, grad_up, grad_down = (
        lax.psum_scatter(
            gate_part.astype(jnp.bfloat16), "seq", scatter_dimension=1, tiled=True
        ).astype(jnp.float32),
        lax.psum_scatter(
            up_part.astype(jnp.bfloat16), "seq", scatter_dimension=1, tiled=True
        ).astype(jnp.float32),
        lax.psum_scatter(
            down_part.astype(jnp.bfloat16), "seq", scatter_dimension=1, tiled=True
        ).astype(jnp.float32),
    )
    return (grad_tokens, grad_route, grad_gate, grad_up, grad_down)


def solution(mesh):
    placed = (
        P(("expert", "seq"), None),
        P(("expert", "seq"), None),
        P(("expert", "seq"), None),
        P(("expert", "seq"), None),
        P("expert", "seq", "tensor"),
        P("expert", "seq", "tensor"),
        P("expert", "seq", "tensor"),
    )
    return jax.shard_map(
        shards,
        mesh=mesh,
        in_specs=placed,
        out_specs=(
            P(("expert", "seq"), "tensor"),
            P(("expert", "seq"), None),
            P("expert", "seq", "tensor"),
            P("expert", "seq", "tensor"),
            P("expert", "seq", "tensor"),
        ),
        check_vma=False,
    )
```

profile of v0, /device:TPU:0, one launch (start us, length us, event | category | flops | bytes accessed | tf_op | source)
XLA Modules:
  0.0 604.1 jit_solution(13995530741329707157)
XLA Ops:
  11.8 2.9 scatter_custom_fusion
  15.7 3.5 gather_fusion
  20.0 8.1 %all-to-all-start = ((bf16[16,1,32]{2,1,0:T(2,128)(2,1)}), bf16[16,1,32]{2,1,0:T(2,128)(2,1)S(1)}, u32[]{:S(2)}, u32[]{:S(2)}) async-start(bf16[16,1,32]{2,1,0:T(2,128)(2,1)} %all_to_all.25), calls=%async_computation | async-start | bytes 16384 | tf_op jit(solution)/shard_map/all_to_all | solution.py:46
  28.2 7.1 %gather_fusion.1 = bf16[512,7168]{1,0:T(8,128)(2,1)} fusion(bf16[192,7168]{1,0:T(8,128)(2,1)S(1)} %copy-done, s32[1024]{0:T(1024)S(1)} %get-tuple-element.29), kind=kCustom, calls=%fused_computation.1 | custom fusion | bytes 14682112 | tf_op jit(solution)/shard_map/gather | solution.py:42
  35.3 15.9 %gather_fusion.2 = bf16[512,7168]{1,0:T(8,128)(2,1)} fusion(bf16[192,7168]{1,0:T(8,128)(2,1)} %param.7, s32[1024]{0:T(1024)S(1)} %get-tuple-element.29), kind=kCustom, calls=%fused_computation.2 | custom fusion | bytes 14682112 | tf_op jit(solution)/shard_map/gather | solution.py:41
  51.2 10.6 %broadcast_multiply_fusion.1 = (bf16[16,32,7168]{2,1,0:T(8,128)(2,1)}, bf16[16,32,7168]{2,1,0:T(8,128)(2,1)}) fusion(bf16[16,32,7168]{2,1,0:T(8,128)(2,1)} %bitcast.67, bf16[16,32]{1,0:T(8,128)(2,1)S(1)} %reshape.301, bf16[16,32,7168]{2,1,0:T(8,128)(2,1)} %bitcast.68), kind=kLoop, calls=%fused_computation.27 | loop fusion | flops 7340032 | bytes 29361152 | tf_op jit(solution)/shard_map/mul | solution.py:42
  61.7 7.3 %all-to-all-start.2 = ((bf16[16,32,7168]{2,1,0:T(8,128)(2,1)}), bf16[16,32,7168]{2,1,0:T(8,128)(2,1)}, u32[]{:S(2)}, u32[]{:S(2)}) async-start(bf16[16,32,7168]{2,1,0:T(8,128)(2,1)} %get-tuple-element.26), calls=%async_computation.2 | async-start | bytes 14680064 | tf_op jit(solution)/shard_map/all_to_all | solution.py:44
  69.8 125.8 %all-to-all-done.2 = bf16[16,32,7168]{2,1,0:T(8,128)(2,1)} async-done(((bf16[16,32,7168]{2,1,0:T(8,128)(2,1)}), bf16[16,32,7168]{2,1,0:T(8,128)(2,1)}, u32[]{:S(2)}, u32[]{:S(2)}) %all-to-all-start.2) | async-done | bytes 7340064 | tf_op jit(solution)/shard_map/all_to_all | solution.py:44
  195.6 4.7 all-to-all-start.1
  201.2 6.2 %fusion.10 = f32[512,256]{0,1:T(8,128)S(1)} fusion(bf16[512,7168]{1,0:T(8,128)(2,1)} %bitcast.5, bf16[1,7168,256]{2,1,0:T(8,128)(2,1)} %all-gather.6.cloned.1.call-done), kind=kOutput, calls=%fused_computation.22 | convolution fusion | flops 1879048192 | bytes 11534336 | tf_op jit(solution)/shard_map/emd,edf->emf/dot_general | solution.py:68
  207.4 6.2 %fusion.7 = f32[512,256]{0,1:T(8,128)S(1)} fusion(bf16[512,7168]{1,0:T(8,128)(2,1)} %bitcast.5, bf16[1,7168,256]{2,1,0:T(8,128)(2,1)} %all-gather.8.cloned.1.call-done), kind=kOutput, calls=%fused_computation.19 | convolution fusion | flops 1879048192 | bytes 11534336 | tf_op jit(solution)/shard_map/emd,edf->emf/dot_general | solution.py:67
  213.7 78.3 %all-gather.4.cloned.1.call-done = bf16[1,7168,256]{2,1,0:T(8,128)(2,1)} async-done(((bf16[1,1792,256]{2,1,0:T(8,128)(2,1)}), bf16[1,7168,256]{2,1,0:T(8,128)(2,1)}) %all-gather.4.cloned.1.call-update) | async-done | bytes 3670032 | tf_op jit(solution)/shard_map/all_gather | solution.py:65
  292.0 33.4 %all-to-all-done.1 = bf16[16,32,7168]{2,1,0:T(8,128)(2,1)} async-done(((bf16[16,32,7168]{2,1,0:T(8,128)(2,1)}), bf16[16,32,7168]{2,1,0:T(8,128)(2,1)}, u32[]{:S(2)}, u32[]{:S(2)}) %all-to-all-start.1) | async-done | bytes 7340064 | tf_op jit(solution)/shard_map/all_to_all | solution.py:45
  325.4 6.6 %multiply_reduce_fusion = (f32[512]{0:T(512)S(1)}, bf16[512,256]{0,1:T(8,128)(2,1)S(1)}, bf16[512,256]{0,1:T(8,128)(2,1)S(1)}) fusion(f32[512,256]{0,1:T(8,128)S(1)} %fusion.10, f32[512,256]{0,1:T(8,128)S(1)} %fusion.7, f32[512]{0:T(512)S(1)} %reshape.300, bf16[512,7168]{1,0:T(8,128)(2,1)} %bitcast.2, bf16[1,7168,256]{2,1,0:T(8,128)(2,1)} %all-gather.4.cloned.1.call-done), kind=kOutput, calls=%fused_computation.30 | convolution fusion | flops 1881275904 | bytes 12587008 | tf_op jit(solution)/shard_map/emd,edf->emf/dot_general | solution.py:73
  332.0 7.4 %fusion.5 = f32[512,7168]{1,0:T(8,128)} fusion(bf16[512,256]{0,1:T(8,128)(2,1)S(1)} %get-tuple-element.23, bf16[1,7168,256]{2,1,0:T(8,128)(2,1)S(1)} %copy-done.3), kind=kOutput, calls=%fused_computation.17 | convolution fusion | flops 1879048192 | bytes 18612224 | tf_op jit(solution)/shard_map/emf,edf->emd/dot_general | solution.py:81
  339.4 10.4 %fusion = bf16[1,512,7168]{2,1,0:T(8,128)(2,1)} fusion(f32[512,7168]{1,0:T(8,128)} %fusion.5, bf16[512,256]{0,1:T(8,128)(2,1)S(1)} %get-tuple-element.24, bf16[1,7168,256]{2,1,0:T(8,128)(2,1)S(1)} %copy-done.2), kind=kOutput, calls=%fused_computation.8 | convolution fusion | flops 1886388224 | bytes 25952256 | tf_op jit(solution)/shard_map/emf,edf->emd/dot_general | solution.py:84
  349.8 31.6 %copy.30 = bf16[1,512,7168]{1,0,2:T(2,128)(2,1)} copy(bf16[1,512,7168]{2,1,0:T(8,128)(2,1)} %fusion) | data formatting | bytes 14680064
  381.4 10.3 %copy.36 = bf16[7168,1,512]{2,0,1:T(8,128)(2,1)} copy(bf16[7168,1,512]{2,1,0:T(2,128)(2,1)} %bitcast.66) | data formatting | bytes 14680064
  391.8 8.0 %fusion.3 = bf16[1,7168,256]{2,1,0:T(8,128)(2,1)} fusion(bf16[512,7168]{1,0:T(8,128)(2,1)} %bitcast.2, f32[512]{0:T(512)S(1)} %reshape.300, f32[512,256]{0,1:T(8,128)S(1)} %fusion.10, f32[512,256]{0,1:T(8,128)S(1)} %fusion.7), kind=kOutput, calls=%fused_computation.14 | convolution fusion | flops 1892679680 | bytes 12060672 | tf_op jit(solution)/shard_map/emd,emf->edf/dot_general | solution.py:112
  399.8 7.1 %fusion.1 = bf16[1,7168,256]{2,1,0:T(8,128)(2,1)} fusion(bf16[512,7168]{1,0:T(8,128)(2,1)} %bitcast.5, bf16[512,256]{0,1:T(8,128)(2,1)S(1)} %get-tuple-element.23), kind=kOutput, calls=%fused_computation.12 | convolution fusion | flops 1880883200 | bytes 11272192 | tf_op jit(solution)/shard_map/emd,emf->edf/dot_general | solution.py:110
  407.0 7.2 %fusion.2 = bf16[1,7168,256]{2,1,0:T(8,128)(2,1)} fusion(bf16[512,7168]{1,0:T(8,128)(2,1)} %bitcast.5, bf16[512,256]{0,1:T(8,128)(2,1)S(1)} %get-tuple-element.24), kind=kOutput, calls=%fused_computation.13 | convolution fusion | flops 1880883200 | bytes 11272192 | tf_op jit(solution)/shard_map/emd,emf->edf/dot_general | solution.py:111
  414.2 24.4 %psum.7 = bf16[1,512]{1,0:T(2,128)(2,1)S(1)} all-reduce(f32[1,512]{1,0:T(1,128)S(1)} %bitcast.71), channel_id=1, replica_groups=mesh['expert'=4,'seq'=4,'tensor'=8] {'tensor'}, use_global_device_ids=true, to_apply=%region_7.8 | all-reduce | flops 512 | bytes 3072 | tf_op jit(solution)/shard_map/psum | solution.py:87
  439.3 3.5 all-to-all-start.4
  444.9 3.3 copy.31
  450.2 5.5 all-to-all-start.3
  455.8 2.8 gather_fusion.4
  459.4 31.7 %reduce-scatter.11.cloned.1.call-done = bf16[1,1792,256]{2,1,0:T(8,128)(2,1)} async-done(((bf16[1,7168,256]{2,1,0:T(8,128)(2,1)}), bf16[1,1792,256]{2,1,0:T(8,128)(2,1)}) %reduce-scatter.11.cloned.1.call-update) | async-done | bytes 917520 | tf_op jit(solution)/shard_map/reduce_scatter | solution.py:120
  493.6 42.0 %reduce-scatter.7.cloned.1.call-done = bf16[1,1792,256]{2,1,0:T(8,128)(2,1)} async-done(((bf16[1,7168,256]{2,1,0:T(8,128)(2,1)}), bf16[1,1792,256]{2,1,0:T(8,128)(2,1)}) %reduce-scatter.7.cloned.1.call-update) | async-done | bytes 917520 | tf_op jit(solution)/shard_map/reduce_scatter | solution.py:114
  538.2 42.1 %reduce-scatter.9.cloned.1.call-done = bf16[1,1792,256]{2,1,0:T(8,128)(2,1)} async-done(((bf16[1,7168,256]{2,1,0:T(8,128)(2,1)}), bf16[1,1792,256]{2,1,0:T(8,128)(2,1)}) %reduce-scatter.9.cloned.1.call-update) | async-done | bytes 917520 | tf_op jit(solution)/shard_map/reduce_scatter | solution.py:117
  585.6 4.7 gather_fusion.3
  590.3 3.0 reshape.298
  593.3 3.7 reduce_sum.33
  (64 shorter events, 24.2 us)
Async XLA Ops:
  7.2 21.0 %copy-start = (bf16[192,7168]{1,0:T(8,128)(2,1)S(1)}, bf16[192,7168]{1,0:T(8,128)(2,1)}, u32[]{:S(2)}) copy-start(bf16[192,7168]{1,0:T(8,128)(2,1)} %param.8) | copy-start | bytes 8257540
  7.2 194.0 %all-gather.6.cloned.1.call-start = ((), (), s32[]{:S(2)}) async-start(), calls=%async_computation.10 | async-start | bytes 4587520 | tf_op jit(solution)/shard_map/all_gather | solution.py:64
  20.0 41.8 %all-to-all-start = ((bf16[16,1,32]{2,1,0:T(2,128)(2,1)}), bf16[16,1,32]{2,1,0:T(2,128)(2,1)S(1)}, u32[]{:S(2)}, u32[]{:S(2)}) async-start(bf16[16,1,32]{2,1,0:T(2,128)(2,1)} %all_to_all.25), calls=%async_computation | async-start | bytes 16384 | tf_op jit(solution)/shard_map/all_to_all | solution.py:46
  61.7 133.8 %all-to-all-start.2 = ((bf16[16,32,7168]{2,1,0:T(8,128)(2,1)}), bf16[16,32,7168]{2,1,0:T(8,128)(2,1)}, u32[]{:S(2)}, u32[]{:S(2)}) async-start(bf16[16,32,7168]{2,1,0:T(8,128)(2,1)} %get-tuple-element.26), calls=%async_computation.2 | async-start | bytes 14680064 | tf_op jit(solution)/shard_map/all_to_all | solution.py:44
  69.0 138.4 %all-gather.8.cloned.1.call-start = ((), (), s32[]{:S(2)}) async-start(), calls=%async_computation.11 | async-start | bytes 4587520 | tf_op jit(solution)/shard_map/all_gather | solution.py:63
  195.6 129.9 %all-to-all-start.1 = ((bf16[16,32,7168]{2,1,0:T(8,128)(2,1)}), bf16[16,32,7168]{2,1,0:T(8,128)(2,1)}, u32[]{:S(2)}, u32[]{:S(2)}) async-start(bf16[16,32,7168]{2,1,0:T(8,128)(2,1)} %get-tuple-element.25), calls=%async_computation.1 | async-start | bytes 14680064 | tf_op jit(solution)/shard_map/all_to_all | solution.py:45
  200.3 91.7 %all-gather.4.cloned.1.call-start = ((), (), s32[]{:S(2)}) async-start(), calls=%async_computation.9 | async-start | bytes 4587520 | tf_op jit(solution)/shard_map/all_gather | solution.py:65
  201.0 241.8 %reduce-scatter.13.cloned.1.call-start = ((), (), s32[]{:S(2)}) async-start(), calls=%async_computation.15 | async-start | bytes 8257536
  325.4 6.6 %copy-start.3 = (bf16[1,7168,256]{2,1,0:T(8,128)(2,1)S(1)}, bf16[1,7168,256]{2,1,0:T(8,128)(2,1)}, u32[]{:S(2)}) copy-start(bf16[1,7168,256]{2,1,0:T(8,128)(2,1)} %all-gather.8.cloned.1.call-done) | copy-start | bytes 11010052
  332.0 7.4 %copy-start.2 = (bf16[1,7168,256]{2,1,0:T(8,128)(2,1)S(1)}, bf16[1,7168,256]{2,1,0:T(8,128)(2,1)}, u32[]{:S(2)}) copy-start(bf16[1,7168,256]{2,1,0:T(8,128)(2,1)} %all-gather.6.cloned.1.call-done) | copy-start | bytes 11010052
  391.8 99.3 %reduce-scatter.11.cloned.1.call-start = ((), (), s32[]{:S(2)}) async-start(), calls=%async_computation.14 | async-start | bytes 4587520 | tf_op jit(solution)/shard_map/reduce_scatter | solution.py:120
  399.8 135.9 %reduce-scatter.7.cloned.1.call-start = ((), (), s32[]{:S(2)}) async-start(), calls=%async_computation.12 | async-start | bytes 4587520 | tf_op jit(solution)/shard_map/reduce_scatter | solution.py:114
  407.0 173.4 %reduce-scatter.9.cloned.1.call-start = ((), (), s32[]{:S(2)}) async-start(), calls=%async_computation.13 | async-start | bytes 4587520 | tf_op jit(solution)/shard_map/reduce_scatter | solution.py:117
  439.3 10.9 %all-to-all-start.4 = ((bf16[16,1,32]{2,1,0:T(2,128)(2,1)}), bf16[16,1,32]{2,1,0:T(2,128)(2,1)S(1)}, u32[]{:S(2)}, u32[]{:S(2)}) async-start(bf16[16,1,32]{2,1,0:T(2,128)(2,1)} %convert_element_type.144), calls=%async_computation.4 | async-start | bytes 16384 | tf_op jit(solution)/shard_map/all_to_all | solution.py:99
  450.2 132.7 %all-to-all-start.3 = ((bf16[16,32,896]{2,1,0:T(8,128)(2,1)}), bf16[16,32,896]{2,1,0:T(8,128)(2,1)}, u32[]{:S(2)}, u32[]{:S(2)}) async-start(bf16[16,32,896]{2,1,0:T(8,128)(2,1)} %bitcast.9), calls=%async_computation.3 | async-start | bytes 1835008 | tf_op jit(solution)/shard_map/all_to_all | solution.py:92
  582.9 14.1 %copy-start.1 = (bf16[192,7168]{1,0:T(8,128)(2,1)S(1)}, bf16[192,7168]{1,0:T(8,128)(2,1)}, u32[]{:S(2)}) copy-start(bf16[192,7168]{1,0:T(8,128)(2,1)} %param.8) | copy-start | bytes 8257540
Sparse Core Ops, SparseCore 0:
  9.7 46.4 all-gather.5
  71.5 90.1 all-gather.7
  202.8 89.1 all-gather.3
  391.9 44.8 reduce-scatter.12
  439.1 51.9 reduce-scatter.10
  493.3 42.2 reduce-scatter.6
  538.1 42.2 reduce-scatter.8
where the time goes:
time: 615 us; the launch traced here: 604 us
  waiting for transfers between devices  358 us (58%)
  local copies, waits for them, and re-layouts  92.3 us (15%)
  matrix products  59 us (10%)
  starting transfers between devices  29.3 us (5%)
  other arithmetic  26.9 us (4%)
  blocking collectives  24.4 us (4%)
  between operations  14.6 us (2%)
    all_to_all x1, waiting for transfers between devices, shards(): lax.all_to_all(in_send, ('expert', 'seq'), split_axis=0, concat_axis=0, t...  126 us
    all_gather x1, waiting for transfers between devices, shards(): lax.all_gather(down_weight, 'seq', axis=1, tiled=True)  78.3 us
    unnamed x15, local copies, waits for them, and re-layouts  49.8 us
    reduce_scatter x1, waiting for transfers between devices, shards(): lax.psum_scatter(up_part.astype(jnp.bfloat16), 'seq', scatter_dimension=1...  42.1 us
    reduce_scatter x1, waiting for transfers between devices, shards(): lax.psum_scatter(gate_part.astype(jnp.bfloat16), 'seq', scatter_dimension...  42 us
    all_to_all x1, waiting for transfers between devices, shards(): lax.all_to_all(out_send, ('expert', 'seq'), split_axis=0, concat_axis=0,...  33.4 us
    reduce_scatter x1, waiting for transfers between devices, shards(): lax.psum_scatter(down_part.astype(jnp.bfloat16), 'seq', scatter_dimension...  31.7 us
    psum x1, blocking collectives, shards(): route_scores = lax.psum(partial_scores, 'tensor')  24.4 us
  transfers between devices with their start and end apart: 12, of which 7 were waited for; matrix products, arithmetic and copies ran while one was open for 16% of the time, Pallas kernels for 0%

commit v1 on v0

--- a/solution.py
+++ b/solution.py
@@ -7,7 +7,8 @@
 def shards(tokens, grad_out, expert_ids, route_weights, gate_weight, up_weight, down_weight):
     expert_count = lax.axis_size("expert")
     seq_count = lax.axis_size("seq")
-    tensor_count = lax.axis_size("tensor")
+    tensor_count = lax.axis_size("tx") * lax.axis_size("core")
+    core = lax.axis_index("core")
     local_count = gate_weight.shape[0]
     tok_rows = tokens.shape[0]
     model_width = tokens.shape[1]
@@ -38,13 +39,25 @@
     weight_send = (
         route_weights.reshape(-1)[safe_source] * filled.astype(route_weights.dtype)
     ).reshape(peer_count, block_rows)
-    in_send = (tokens[token_of] * keep).reshape(peer_count, block_rows, model_width)
-    out_send = (grad_out[token_of] * keep).reshape(peer_count, block_rows, model_width)
-    in_recv, out_recv, weight_recv = (
+    half = model_width // 2
+    tokens_half = lax.dynamic_slice_in_dim(tokens, core * half, half, axis=1)
+    grad_half = lax.dynamic_slice_in_dim(grad_out, core * half, half, axis=1)
+    in_send = (tokens_half[token_of] * keep).reshape(peer_count, block_rows, half)
+    out_send = (grad_half[token_of] * keep).reshape(peer_count, block_rows, half)
+    in_mine, out_mine, weight_recv = (
         lax.all_to_all(in_send, ("expert", "seq"), split_axis=0, concat_axis=0, tiled=True),
         lax.all_to_all(out_send, ("expert", "seq"), split_axis=0, concat_axis=0, tiled=True),
         lax.all_to_all(weight_send, ("expert", "seq"), split_axis=0, concat_axis=0, tiled=True),
     )
+
+    def join_halves(mine):
+        other = lax.ppermute(mine, "core", [(0, 1), (1, 0)])
+        first = jnp.where(core == 0, mine, other)
+        second = jnp.where(core == 0, other, mine)
+        return jnp.concatenate([first, second], axis=-1)
+
+    in_recv = join_halves(in_mine)
+    out_recv = join_halves(out_mine)
 
     def by_expert(values):
         shaped = values.reshape((peer_count, local_count, per_peer) + values.shape[2:])
@@ -84,9 +97,9 @@
     input_terms = input_terms + jnp.einsum(
         "emf,edf->emd", up_grad, up_full, preferred_element_type=jnp.float32
     )
-    route_scores = lax.psum(partial_scores, "tensor")
+    route_scores = lax.psum(partial_scores, ("tx", "core"))
     input_shards = lax.psum_scatter(
-        input_terms.astype(jnp.bfloat16), "tensor", scatter_dimension=2, tiled=True
+        input_terms.astype(jnp.bfloat16), ("tx", "core"), scatter_dimension=2, tiled=True
     ).astype(jnp.float32)
     back_rows, back_scores = (
         lax.all_to_all(
@@ -125,25 +138,30 @@
 
 
 def solution(mesh):
+    shape = mesh.devices.shape
+    mesh = jax.sharding.Mesh(
+        mesh.devices.reshape(shape[0], shape[1], shape[2] // 2, 2), ("expert", "seq", "tx", "core")
+    )
+    tensor = ("tx", "core")
     placed = (
         P(("expert", "seq"), None),
         P(("expert", "seq"), None),
         P(("expert", "seq"), None),
         P(("expert", "seq"), None),
-        P("expert", "seq", "tensor"),
-        P("expert", "seq", "tensor"),
-        P("expert", "seq", "tensor"),
+        P("expert", "seq", tensor),
+        P("expert", "seq", tensor),
+        P("expert", "seq", tensor),
     )
     return jax.shard_map(
         shards,
         mesh=mesh,
         in_specs=placed,
         out_specs=(
-            P(("expert", "seq"), "tensor"),
+            P(("expert", "seq"), tensor),
             P(("expert", "seq"), None),
-            P("expert", "seq", "tensor"),
-            P("expert", "seq", "tensor"),
-            P("expert", "seq", "tensor"),
+            P("expert", "seq", tensor),
+            P("expert", "seq", tensor),
+            P("expert", "seq", tensor),
         ),
         check_vma=False,
     )

time: 615 us -> 519 us (0.84)
  waiting for transfers between devices: 358 us -> 258 us
  local copies, waits for them, and re-layouts: 92.3 us -> 74 us
  blocking collectives: 24.4 us -> 40.2 us
  other arithmetic: 26.9 us -> 42 us
  starting transfers between devices: 29.3 us -> 22.7 us
    all_gather x1, waiting for transfers between devices: 78.3 us -> 0.01 us  [shards(): lax.all_gather(down_weight, 'seq', axis=1, tiled=True)]
    all_to_all x1, waiting for transfers between devices: 126 us -> 71.5 us  [shards(): lax.all_to_all(in_send, ('expert', 'seq'), split_axis=0, concat_axis=0, t...]
    all_to_all x1, waiting for transfers between devices: 33.4 us -> 69.7 us  [shards(): lax.all_to_all(out_send, ('expert', 'seq'), split_axis=0, concat_axis=0,...]
    gather x2, local copies, waits for them, and re-layouts: 23 us -> 8.37 us  [the longest x1 4.2 us: shards(): tokens_half[token_of] * keep]
    all_to_all x0 -> x1, blocking collectives: none -> 13 us  [shards(): lax.all_to_all(weight_send, ('expert', 'seq'), split_axis=0, concat_axis=...]
    concatenate x0 -> x2, other arithmetic: none -> 11.5 us  [join_halves(): return jnp.concatenate([first, second], axis=-1)]
    select_n x0 -> x2, other arithmetic: none -> 11 us  [join_halves(): first = jnp.where(core == 0, mine, other)]
    all_to_all x1 -> x0, starting transfers between devices: 8.13 us -> none  [shards(): lax.all_to_all(weight_send, ('expert', 'seq'), split_axis=0, concat_axis=...]
  transfers between devices with their start and end apart: 12 -> 13, of which waited for: 7 -> 6; matrix products, arithmetic and copies ran while one was open for 16% -> 20% of each run, Pallas kernels for 0% -> 0%
where the time goes in v1:
time: 519 us; the launch traced here: 511 us
  waiting for transfers between devices  258 us (50%)
  local copies, waits for them, and re-layouts  74 us (14%)
  matrix products  59.2 us (11%)
  other arithmetic  42 us (8%)
  blocking collectives  40.2 us (8%)
  starting transfers between devices  22.7 us (4%)
  between operations  14.6 us (3%)
    all_to_all x1, waiting for transfers between devices, shards(): lax.all_to_all(in_send, ('expert', 'seq'), split_axis=0, concat_axis=0, t...  71.5 us
    all_to_all x1, waiting for transfers between devices, shards(): lax.all_to_all(out_send, ('expert', 'seq'), split_axis=0, concat_axis=0,...  69.7 us
    unnamed x11, local copies, waits for them, and re-layouts  49.6 us
    reduce_scatter x1, waiting for transfers between devices, shards(): lax.psum_scatter(up_part.astype(jnp.bfloat16), 'seq', scatter_dimension=1...  42.1 us
    reduce_scatter x1, waiting for transfers between devices, shards(): lax.psum_scatter(gate_part.astype(jnp.bfloat16), 'seq', scatter_dimension...  41.9 us
    reduce_scatter x1, waiting for transfers between devices, shards(): lax.psum_scatter(down_part.astype(jnp.bfloat16), 'seq', scatter_dimension...  28.8 us
    psum x1, blocking collectives, shards(): route_scores = lax.psum(partial_scores, ('tx', 'core'))  27.2 us
    all_to_all x1, blocking collectives, shards(): lax.all_to_all(weight_send, ('expert', 'seq'), split_axis=0, concat_axis=...  13 us
  transfers between devices with their start and end apart: 13, of which 6 were waited for; matrix products, arithmetic and copies ran while one was open for 20% of the time, Pallas kernels for 0%

profile of v1, /device:TPU:0, one launch (start us, length us, event | category | flops | bytes accessed | tf_op | source)
XLA Modules:
  0.0 510.7 jit_solution(3057996658511665825)
XLA Ops:
  12.7 2.9 scatter_custom_fusion
  15.7 3.5 gather_fusion
  21.4 4.2 gather_fusion.2
  25.6 4.2 gather_fusion.1
  29.7 6.8 %broadcast_multiply_fusion.1 = (bf16[16,32,3584]{2,1,0:T(8,128)(2,1)}, bf16[16,32,3584]{2,1,0:T(8,128)(2,1)}) fusion(bf16[16,32,3584]{2,1,0:T(8,128)(2,1)} %bitcast.74, bf16[16,32]{1,0:T(8,128)(2,1)S(1)} %reshape.301, bf16[16,32,3584]{2,1,0:T(8,128)(2,1)} %bitcast.73), kind=kLoop, calls=%fused_computation.34 | loop fusion | flops 3670016 | bytes 14681088 | tf_op jit(solution)/shard_map/mul | solution.py:46
  36.5 8.3 %all-to-all-start.2 = ((bf16[16,32,3584]{2,1,0:T(8,128)(2,1)}), bf16[16,32,3584]{2,1,0:T(8,128)(2,1)}, u32[]{:S(2)}, u32[]{:S(2)}) async-start(bf16[16,32,3584]{2,1,0:T(8,128)(2,1)} %get-tuple-element.30), calls=%async_computation.2 | async-start | bytes 7340032 | tf_op jit(solution)/shard_map/all_to_all | solution.py:48
  45.6 71.5 %all-to-all-done.2 = bf16[16,32,3584]{2,1,0:T(8,128)(2,1)} async-done(((bf16[16,32,3584]{2,1,0:T(8,128)(2,1)}), bf16[16,32,3584]{2,1,0:T(8,128)(2,1)}, u32[]{:S(2)}, u32[]{:S(2)}) %all-to-all-start.2) | async-done | bytes 3670048 | tf_op jit(solution)/shard_map/all_to_all | solution.py:48
  117.1 13.0 %all_to_all.31 = bf16[16,1,32]{2,1,0:T(2,128)(2,1)S(1)} all-to-all(bf16[16,1,32]{2,1,0:T(2,128)(2,1)S(1)} %all_to_all.25), channel_id=1, replica_groups=mesh['expert'=4,'seq'=4,'tx'=4,'core'=2] {'expert','seq'}, dimensions={0} | all-to-all | bytes 2048 | tf_op jit(solution)/shard_map/all_to_all | solution.py:50
  130.1 4.5 all-to-all-start.1
  135.6 69.7 %all-to-all-done.1 = bf16[16,32,3584]{2,1,0:T(8,128)(2,1)} async-done(((bf16[16,32,3584]{2,1,0:T(8,128)(2,1)}), bf16[16,32,3584]{2,1,0:T(8,128)(2,1)}, u32[]{:S(2)}, u32[]{:S(2)}) %all-to-all-start.1) | async-done | bytes 3670048 | tf_op jit(solution)/shard_map/all_to_all | solution.py:49
  205.7 5.4 %broadcast_select_fusion.1 = (bf16[16,32,3584]{2,1,0:T(8,128)(2,1)S(1)}, bf16[16,32,3584]{2,1,0:T(8,128)(2,1)}) fusion(bf16[16,32,3584]{2,1,0:T(8,128)(2,1)} %all-to-all-done.2, bf16[16,32,3584]{2,1,0:T(8,128)(2,1)} %collective-permute-done.1, pred[]{:T(512)S(6)} %eq.42), kind=kLoop, calls=%fused_computation.29 | loop fusion | flops 3670016 | bytes 14680065 | tf_op jit(solution)/shard_map/jit(_where)/select_n | solution.py:55
  211.1 5.8 %pad_maximum_fusion.1 = bf16[16,32,7168]{2,1,0:T(8,128)(2,1)} fusion(bf16[16,32,3584]{2,1,0:T(8,128)(2,1)} %get-tuple-element.25, bf16[16,32,3584]{2,1,0:T(8,128)(2,1)S(1)} %get-tuple-element.24), kind=kLoop, calls=%fused_computation.16 | loop fusion | flops 14680064 | bytes 14680064 | tf_op jit(solution)/shard_map/concatenate | solution.py:57
  216.9 6.2 %fusion.7 = f32[512,256]{0,1:T(8,128)S(1)} fusion(bf16[512,7168]{1,0:T(8,128)(2,1)} %bitcast.67, bf16[1,7168,256]{2,1,0:T(8,128)(2,1)} %all-gather.8.cloned.1.call-done), kind=kOutput, calls=%fused_computation.21 | convolution fusion | flops 1879048192 | bytes 11534336 | tf_op jit(solution)/shard_map/emd,edf->emf/dot_general | solution.py:80
  223.1 6.2 %fusion.10 = f32[512,256]{0,1:T(8,128)S(1)} fusion(bf16[512,7168]{1,0:T(8,128)(2,1)} %bitcast.68, bf16[1,7168,256]{2,1,0:T(8,128)(2,1)} %all-gather.6.cloned.1.call-done), kind=kOutput, calls=%fused_computation.24 | convolution fusion | flops 1879048192 | bytes 11534336 | tf_op jit(solution)/shard_map/emd,edf->emf/dot_general | solution.py:81
  229.4 5.6 %broadcast_select_fusion.3 = (bf16[16,32,3584]{2,1,0:T(8,128)(2,1)S(1)}, bf16[16,32,3584]{2,1,0:T(8,128)(2,1)}) fusion(bf16[16,32,3584]{2,1,0:T(8,128)(2,1)} %all-to-all-done.1, bf16[16,32,3584]{2,1,0:T(8,128)(2,1)} %collective-permute-done, pred[]{:T(512)S(6)} %eq.42), kind=kLoop, calls=%fused_computation.31 | loop fusion | flops 3670016 | bytes 14680065 | tf_op jit(solution)/shard_map/jit(_where)/select_n | solution.py:55
  234.9 5.8 %pad_maximum_fusion = bf16[16,32,7168]{2,1,0:T(8,128)(2,1)} fusion(bf16[16,32,3584]{2,1,0:T(8,128)(2,1)} %get-tuple-element.23, bf16[16,32,3584]{2,1,0:T(8,128)(2,1)S(1)} %get-tuple-element.22), kind=kLoop, calls=%fused_computation.15 | loop fusion | flops 14680064 | bytes 14680064 | tf_op jit(solution)/shard_map/concatenate | solution.py:57
  240.7 6.6 %multiply_reduce_fusion = (f32[512]{0:T(512)S(1)}, bf16[512,256]{0,1:T(8,128)(2,1)S(1)}, bf16[512,256]{0,1:T(8,128)(2,1)S(1)}) fusion(f32[512,256]{0,1:T(8,128)S(1)} %fusion.10, f32[512,256]{0,1:T(8,128)S(1)} %fusion.7, f32[512]{0:T(512)S(1)} %reshape.300, bf16[512,7168]{1,0:T(8,128)(2,1)} %bitcast.75, bf16[1,7168,256]{2,1,0:T(8,128)(2,1)} %all-gather.4.cloned.1.call-done), kind=kOutput, calls=%fused_computation.36 | convolution fusion | flops 1881275904 | bytes 12587008 | tf_op jit(solution)/shard_map/emd,edf->emf/dot_general | solution.py:86
  247.3 7.4 %fusion.5 = f32[512,7168]{1,0:T(8,128)} fusion(bf16[512,256]{0,1:T(8,128)(2,1)S(1)} %get-tuple-element.27, bf16[1,7168,256]{2,1,0:T(8,128)(2,1)S(1)} %copy-done.1), kind=kOutput, calls=%fused_computation.19 | convolution fusion | flops 1879048192 | bytes 18612224 | tf_op jit(solution)/shard_map/emf,edf->emd/dot_general | solution.py:94
  254.7 10.6 %fusion = bf16[1,512,7168]{2,1,0:T(8,128)(2,1)} fusion(f32[512,7168]{1,0:T(8,128)} %fusion.5, bf16[512,256]{0,1:T(8,128)(2,1)S(1)} %get-tuple-element.28, bf16[1,7168,256]{2,1,0:T(8,128)(2,1)S(1)} %copy-done), kind=kOutput, calls=%fused_computation.8 | convolution fusion | flops 1886388224 | bytes 25952256 | tf_op jit(solution)/shard_map/emf,edf->emd/dot_general | solution.py:97
  265.3 31.4 %copy.30 = bf16[1,512,7168]{1,0,2:T(2,128)(2,1)} copy(bf16[1,512,7168]{2,1,0:T(8,128)(2,1)} %fusion) | data formatting | bytes 14680064
  296.7 10.3 %copy.36 = bf16[7168,1,512]{2,0,1:T(8,128)(2,1)} copy(bf16[7168,1,512]{2,1,0:T(2,128)(2,1)} %bitcast.71) | data formatting | bytes 14680064
  307.1 8.0 %fusion.3 = bf16[1,7168,256]{2,1,0:T(8,128)(2,1)} fusion(bf16[512,7168]{1,0:T(8,128)(2,1)} %bitcast.76, f32[512]{0:T(512)S(1)} %reshape.300, f32[512,256]{0,1:T(8,128)S(1)} %fusion.10, f32[512,256]{0,1:T(8,128)S(1)} %fusion.7), kind=kOutput, calls=%fused_computation.14 | convolution fusion | flops 1892679680 | bytes 12060672 | tf_op jit(solution)/shard_map/emd,emf->edf/dot_general | solution.py:125
  315.2 7.1 %fusion.1 = bf16[1,7168,256]{2,1,0:T(8,128)(2,1)} fusion(bf16[512,7168]{1,0:T(8,128)(2,1)} %bitcast.69, bf16[512,256]{0,1:T(8,128)(2,1)S(1)} %get-tuple-element.27), kind=kOutput, calls=%fused_computation.12 | convolution fusion | flops 1880883200 | bytes 11272192 | tf_op jit(solution)/shard_map/emd,emf->edf/dot_general | solution.py:123
  322.4 7.2 %fusion.2 = bf16[1,7168,256]{2,1,0:T(8,128)(2,1)} fusion(bf16[512,7168]{1,0:T(8,128)(2,1)} %bitcast.70, bf16[512,256]{0,1:T(8,128)(2,1)S(1)} %get-tuple-element.28), kind=kOutput, calls=%fused_computation.13 | convolution fusion | flops 1880883200 | bytes 11272192 | tf_op jit(solution)/shard_map/emd,emf->edf/dot_general | solution.py:124
  329.5 27.2 %psum.7 = bf16[1,512]{1,0:T(2,128)(2,1)S(1)} all-reduce(f32[1,512]{1,0:T(1,128)S(1)} %bitcast.78), channel_id=1, replica_groups=mesh['expert'=4,'seq'=4,'tx'=4,'core'=2] {'tx','core'}, use_global_device_ids=true, to_apply=%region_7.8 | all-reduce | flops 512 | bytes 3072 | tf_op jit(solution)/shard_map/psum | solution.py:100
  357.4 3.7 all-to-all-start.4
  363.3 3.4 copy.31
  368.5 5.4 %all-to-all-start.3 = ((bf16[16,32,896]{2,1,0:T(8,128)(2,1)}), bf16[16,32,896]{2,1,0:T(8,128)(2,1)S(1)}, u32[]{:S(2)}, u32[]{:S(2)}) async-start(bf16[16,32,896]{2,1,0:T(8,128)(2,1)} %bitcast.9), calls=%async_computation.3 | async-start | bytes 1835008 | tf_op jit(solution)/shard_map/all_to_all | solution.py:105
  374.0 2.8 gather_fusion.4
  377.6 28.8 %reduce-scatter.11.cloned.1.call-done = bf16[1,1792,256]{2,1,0:T(8,128)(2,1)} async-done(((bf16[1,7168,256]{2,1,0:T(8,128)(2,1)}), bf16[1,1792,256]{2,1,0:T(8,128)(2,1)}) %reduce-scatter.11.cloned.1.call-update) | async-done | bytes 917520 | tf_op jit(solution)/shard_map/reduce_scatter | solution.py:133
  409.0 41.9 %reduce-scatter.7.cloned.1.call-done = bf16[1,1792,256]{2,1,0:T(8,128)(2,1)} async-done(((bf16[1,7168,256]{2,1,0:T(8,128)(2,1)}), bf16[1,1792,256]{2,1,0:T(8,128)(2,1)}) %reduce-scatter.7.cloned.1.call-update) | async-done | bytes 917520 | tf_op jit(solution)/shard_map/reduce_scatter | solution.py:127
  453.5 42.1 %reduce-scatter.9.cloned.1.call-done = bf16[1,1792,256]{2,1,0:T(8,128)(2,1)} async-done(((bf16[1,7168,256]{2,1,0:T(8,128)(2,1)}), bf16[1,1792,256]{2,1,0:T(8,128)(2,1)}) %reduce-scatter.9.cloned.1.call-update) | async-done | bytes 917520 | tf_op jit(solution)/shard_map/reduce_scatter | solution.py:130
  (68 shorter events, 28.7 us)
Async XLA Ops:
  7.2 209.7 %all-gather.8.cloned.1.call-start = ((), (), s32[]{:S(2)}) async-start(), calls=%async_computation.11 | async-start | bytes 4587520 | tf_op jit(solution)/shard_map/all_gather | solution.py:76
  36.5 80.6 %all-to-all-start.2 = ((bf16[16,32,3584]{2,1,0:T(8,128)(2,1)}), bf16[16,32,3584]{2,1,0:T(8,128)(2,1)}, u32[]{:S(2)}, u32[]{:S(2)}) async-start(bf16[16,32,3584]{2,1,0:T(8,128)(2,1)} %get-tuple-element.30), calls=%async_computation.2 | async-start | bytes 7340032 | tf_op jit(solution)/shard_map/all_to_all | solution.py:48
  44.8 178.3 %all-gather.6.cloned.1.call-start = ((), (), s32[]{:S(2)}) async-start(), calls=%async_computation.10 | async-start | bytes 4587520 | tf_op jit(solution)/shard_map/all_gather | solution.py:77
  117.1 88.6 %collective-permute-start.1 = (bf16[16,32,3584]{2,1,0:T(8,128)(2,1)}, bf16[16,32,3584]{2,1,0:T(8,128)(2,1)}, u32[]{:S(2)}, u32[]{:S(2)}) collective-permute-start(bf16[16,32,3584]{2,1,0:T(8,128)(2,1)} %all-to-all-done.2), channel_id=1, source_target_pairs={{0,1},{1,0},{2,3},{3,2},{4,5},{5,4},{6,7},{7,6},{8,9},{9,8},{10,11... | collective-permute-start | bytes 11010056 | tf_op jit(solution)/shard_map/ppermute | solution.py:54
  130.1 75.1 %all-to-all-start.1 = ((bf16[16,32,3584]{2,1,0:T(8,128)(2,1)}), bf16[16,32,3584]{2,1,0:T(8,128)(2,1)}, u32[]{:S(2)}, u32[]{:S(2)}) async-start(bf16[16,32,3584]{2,1,0:T(8,128)(2,1)} %get-tuple-element.29), calls=%async_computation.1 | async-start | bytes 7340032 | tf_op jit(solution)/shard_map/all_to_all | solution.py:49
  134.7 106.0 %all-gather.4.cloned.1.call-start = ((), (), s32[]{:S(2)}) async-start(), calls=%async_computation.9 | async-start | bytes 4587520 | tf_op jit(solution)/shard_map/all_gather | solution.py:78
  135.4 225.7 %reduce-scatter.13.cloned.1.call-start = ((), (), s32[]{:S(2)}) async-start(), calls=%async_computation.15 | async-start | bytes 8257536
  205.2 24.1 %collective-permute-start = (bf16[16,32,3584]{2,1,0:T(8,128)(2,1)}, bf16[16,32,3584]{2,1,0:T(8,128)(2,1)}, u32[]{:S(2)}, u32[]{:S(2)}) collective-permute-start(bf16[16,32,3584]{2,1,0:T(8,128)(2,1)} %all-to-all-done.1), channel_id=1, source_target_pairs={{0,1},{1,0},{2,3},{3,2},{4,5},{5,4},{6,7},{7,6},{8,9},{9,8},{10,11... | collective-permute-start | bytes 11010056 | tf_op jit(solution)/shard_map/ppermute | solution.py:54
  240.7 6.6 %copy-start.1 = (bf16[1,7168,256]{2,1,0:T(8,128)(2,1)S(1)}, bf16[1,7168,256]{2,1,0:T(8,128)(2,1)}, u32[]{:S(2)}) copy-start(bf16[1,7168,256]{2,1,0:T(8,128)(2,1)} %all-gather.8.cloned.1.call-done) | copy-start | bytes 11010052
  247.3 7.4 %copy-start = (bf16[1,7168,256]{2,1,0:T(8,128)(2,1)S(1)}, bf16[1,7168,256]{2,1,0:T(8,128)(2,1)}, u32[]{:S(2)}) copy-start(bf16[1,7168,256]{2,1,0:T(8,128)(2,1)} %all-gather.6.cloned.1.call-done) | copy-start | bytes 11010052
  307.1 99.3 %reduce-scatter.11.cloned.1.call-start = ((), (), s32[]{:S(2)}) async-start(), calls=%async_computation.14 | async-start | bytes 4587520 | tf_op jit(solution)/shard_map/reduce_scatter | solution.py:133
  315.1 135.8 %reduce-scatter.7.cloned.1.call-start = ((), (), s32[]{:S(2)}) async-start(), calls=%async_computation.12 | async-start | bytes 4587520 | tf_op jit(solution)/shard_map/reduce_scatter | solution.py:127
  322.3 173.3 %reduce-scatter.9.cloned.1.call-start = ((), (), s32[]{:S(2)}) async-start(), calls=%async_computation.13 | async-start | bytes 4587520 | tf_op jit(solution)/shard_map/reduce_scatter | solution.py:130
  357.4 11.1 %all-to-all-start.4 = ((bf16[16,1,32]{2,1,0:T(2,128)(2,1)}), bf16[16,1,32]{2,1,0:T(2,128)(2,1)S(1)}, u32[]{:S(2)}, u32[]{:S(2)}) async-start(bf16[16,1,32]{2,1,0:T(2,128)(2,1)} %convert_element_type.144), calls=%async_computation.4 | async-start | bytes 16384 | tf_op jit(solution)/shard_map/all_to_all | solution.py:112
  368.5 129.6 %all-to-all-start.3 = ((bf16[16,32,896]{2,1,0:T(8,128)(2,1)}), bf16[16,32,896]{2,1,0:T(8,128)(2,1)S(1)}, u32[]{:S(2)}, u32[]{:S(2)}) async-start(bf16[16,32,896]{2,1,0:T(8,128)(2,1)} %bitcast.9), calls=%async_computation.3 | async-start | bytes 1835008 | tf_op jit(solution)/shard_map/all_to_all | solution.py:105
Sparse Core Ops, SparseCore 0:
  9.7 68.4 all-gather.7
  79.8 54.8 all-gather.5
  137.2 69.4 all-gather.3
  307.2 44.7 reduce-scatter.12
  354.3 52.0 reduce-scatter.10
  408.7 42.1 reduce-scatter.6
  453.3 42.2 reduce-scatter.8

commit v2 on v1

--- a/solution.py
+++ b/solution.py
@@ -51,13 +51,8 @@
     )
 
     def join_halves(mine):
-        other = lax.ppermute(mine, "core", [(0, 1), (1, 0)])
-        first = jnp.where(core == 0, mine, other)
-        second = jnp.where(core == 0, other, mine)
-        return jnp.concatenate([first, second], axis=-1)
-
-    in_recv = join_halves(in_mine)
-    out_recv = join_halves(out_mine)
+        both = jnp.broadcast_to(mine[None], (2,) + mine.shape)
+        return lax.all_to_all(both, "core", split_axis=0, concat_axis=0, tiled=True)
 
     def by_expert(values):
         shaped = values.reshape((peer_count, local_count, per_peer) + values.shape[2:])
@@ -69,70 +64,73 @@
         shaped = values.reshape((local_count, peer_count, per_peer) + values.shape[2:])
         return jnp.swapaxes(shaped, 0, 1).reshape((peer_count, block_rows) + values.shape[2:])
 
-    in_rows = by_expert(in_recv)
-    out_rows = by_expert(out_recv)
+    in_rows = jax.vmap(by_expert)(join_halves(in_mine))
+    out_rows = jax.vmap(by_expert)(join_halves(out_mine))
     prob = by_expert(weight_recv).astype(jnp.float32)[:, :, None]
     gate_full, up_full, down_full = (
         lax.all_gather(gate_weight, "seq", axis=1, tiled=True),
         lax.all_gather(up_weight, "seq", axis=1, tiled=True),
         lax.all_gather(down_weight, "seq", axis=1, tiled=True),
     )
-    pre_gate = jnp.einsum("emd,edf->emf", in_rows, gate_full, preferred_element_type=jnp.float32)
-    pre_up = jnp.einsum("emd,edf->emf", in_rows, up_full, preferred_element_type=jnp.float32)
+    hidden_count = gate_full.shape[2]
+    gate_h, up_h, down_h = (
+        w.reshape(local_count, 2, half, hidden_count) for w in (gate_full, up_full, down_full)
+    )
+    pre_gate = jnp.einsum("cemd,ecdf->emf", in_rows, gate_h, preferred_element_type=jnp.float32)
+    pre_up = jnp.einsum("cemd,ecdf->emf", in_rows, up_h, preferred_element_type=jnp.float32)
     sigmoid_gate = jax.nn.sigmoid(pre_gate)
     silu_gate = pre_gate * sigmoid_gate
     hidden = silu_gate * pre_up
     hidden_low = hidden.astype(jnp.bfloat16)
-    back_proj = jnp.einsum("emd,edf->emf", out_rows, down_full, preferred_element_type=jnp.float32)
+    back_proj = jnp.einsum("cemd,ecdf->emf", out_rows, down_h, preferred_element_type=jnp.float32)
     partial_scores = jnp.sum(hidden * back_proj, axis=2)
-    scaled = (prob * out_rows.astype(jnp.float32)).astype(jnp.bfloat16)
+    scaled = (prob[None] * out_rows.astype(jnp.float32)).astype(jnp.bfloat16)
     hidden_grad = prob * back_proj
     up_grad = (hidden_grad * silu_gate).astype(jnp.bfloat16)
     gate_grad = (
         hidden_grad * pre_up * sigmoid_gate * (1.0 + pre_gate * (1.0 - sigmoid_gate))
     ).astype(jnp.bfloat16)
     input_terms = jnp.einsum(
-        "emf,edf->emd", gate_grad, gate_full, preferred_element_type=jnp.float32
+        "emf,ecdf->ecdm", gate_grad, gate_h, preferred_element_type=jnp.float32
     )
     input_terms = input_terms + jnp.einsum(
-        "emf,edf->emd", up_grad, up_full, preferred_element_type=jnp.float32
+        "emf,ecdf->ecdm", up_grad, up_h, preferred_element_type=jnp.float32
     )
-    route_scores = lax.psum(partial_scores, ("tx", "core"))
-    input_shards = lax.psum_scatter(
-        input_terms.astype(jnp.bfloat16), ("tx", "core"), scatter_dimension=2, tiled=True
+    rows_here = local_count * slot_count
+    input_terms = jnp.swapaxes(
+        input_terms.reshape(local_count, tensor_count, part_width, slot_count), 0, 1
+    ).reshape(tensor_count, part_width, rows_here)
+    score_pad = 16
+    score_rows = jnp.zeros((tensor_count, score_pad, rows_here), jnp.float32)
+    score_rows = score_rows.at[:, 0, :].set(partial_scores.reshape(1, rows_here))
+    stacked = jnp.concatenate([input_terms, score_rows], axis=1).astype(jnp.bfloat16)
+    reduced = lax.psum_scatter(
+        stacked.reshape(tensor_count * (part_width + score_pad), rows_here),
+        ("tx", "core"),
+        scatter_dimension=0,
+        tiled=True,
+    )
+    back_send = by_peer(
+        jnp.swapaxes(reduced, 0, 1).reshape(local_count, slot_count, part_width + score_pad)
+    )
+    back_all = lax.all_to_all(
+        back_send, ("expert", "seq"), split_axis=0, concat_axis=0, tiled=True
     ).astype(jnp.float32)
-    back_rows, back_scores = (
-        lax.all_to_all(
-            by_peer(input_shards).astype(jnp.bfloat16),
-            ("expert", "seq"),
-            split_axis=0,
-            concat_axis=0,
-            tiled=True,
-        ).astype(jnp.float32),
-        lax.all_to_all(
-            by_peer(route_scores).astype(jnp.bfloat16),
-            ("expert", "seq"),
-            split_axis=0,
-            concat_axis=0,
-            tiled=True,
-        ).astype(jnp.float32),
-    )
-    route_rows = back_rows.reshape(slot_count, part_width)[target].reshape(tok_rows, 2, part_width)
+    back_all = back_all.reshape(slot_count, part_width + score_pad)[target]
+    route_rows = back_all[:, :part_width].reshape(tok_rows, 2, part_width)
     grad_tokens = jnp.sum(route_rows, axis=1).astype(jnp.bfloat16)
-    grad_route = back_scores.reshape(slot_count)[target].reshape(tok_rows, 2)
-    gate_part = jnp.einsum("emd,emf->edf", in_rows, gate_grad, preferred_element_type=jnp.float32)
-    up_part = jnp.einsum("emd,emf->edf", in_rows, up_grad, preferred_element_type=jnp.float32)
-    down_part = jnp.einsum("emd,emf->edf", scaled, hidden_low, preferred_element_type=jnp.float32)
+    grad_route = back_all[:, part_width].reshape(tok_rows, 2)
+    gate_part = jnp.einsum("cemd,emf->ecdf", in_rows, gate_grad, preferred_element_type=jnp.float32)
+    up_part = jnp.einsum("cemd,emf->ecdf", in_rows, up_grad, preferred_element_type=jnp.float32)
+    down_part = jnp.einsum("cemd,emf->ecdf", scaled, hidden_low, preferred_element_type=jnp.float32)
     grad_gate, grad_up, grad_down = (
         lax.psum_scatter(
-            gate_part.astype(jnp.bfloat16), "seq", scatter_dimension=1, tiled=True
-        ).astype(jnp.float32),
-        lax.psum_scatter(
-            up_part.astype(jnp.bfloat16), "seq", scatter_dimension=1, tiled=True
-        ).astype(jnp.float32),
-        lax.psum_scatter(
-            down_part.astype(jnp.bfloat16), "seq", scatter_dimension=1, tiled=True
-        ).astype(jnp.float32),
+            part.reshape(local_count, model_width, hidden_count).astype(jnp.bfloat16),
+            "seq",
+            scatter_dimension=1,
+            tiled=True,
+        ).astype(jnp.float32)
+        for part in (gate_part, up_part, down_part)
     )
     return (grad_tokens, grad_route, grad_gate, grad_up, grad_down)
 

time: 519 us -> 488 us (0.940); the launches traced: 511 us -> 486 us
  blocking collectives: 40.2 us -> 10.9 us
  waiting for transfers between devices: 258 us -> 270 us
  starting transfers between devices: 22.7 us -> 31.1 us
  other arithmetic: 42 us -> 34.7 us
  local copies, waits for them, and re-layouts: 74 us -> 66.9 us
    unnamed x11 -> x7, local copies, waits for them, and re-layouts: 49.6 us -> 2.3 us
    psum x1 -> x0, blocking collectives: 27.2 us -> none  [shards(): route_scores = lax.psum(partial_scores, ('tx', 'core'))]
    dot_general x0 -> x2, local copies, waits for them, and re-layouts: none -> 20.2 us  [the longest x1 10.2 us: shards(): jnp.einsum('cemd,emf->ecdf', in_rows, gate_grad, preferred_element_type=j...]
    reduce_scatter x3 -> x4, waiting for transfers between devices: 113 us -> 130 us  [the longest x3 130 us: shards(): lax.psum_scatter(part.reshape(local_count, model_width, hidden_count).ast...]
    select_n x2 -> x0, other arithmetic: 11 us -> none  [join_halves(): first = jnp.where(core == 0, mine, other)]
    add x0 -> x1, local copies, waits for them, and re-layouts: none -> 9.95 us  [shards(): input_terms + jnp.einsum('emf,ecdf->ecdm', up_grad, up_h, preferred_eleme...]
    all_to_all x2 -> x3, starting transfers between devices: 9.07 us -> 18.6 us  [the longest x1 8.13 us: shards(): lax.all_to_all(weight_send, ('expert', 'seq'), split_axis=0, concat_axis=...]
    broadcast_in_dim x0 -> x2, local copies, waits for them, and re-layouts: none -> 8.71 us  [join_halves(): both = jnp.broadcast_to(mine[None], (2,) + mine.shape)]
  transfers between devices with their start and end apart: 13 -> 12, of which waited for: 6 -> 6; matrix products, arithmetic and copies ran while one was open for 20% -> 23% of each run, Pallas kernels for 0% -> 0%
where the time goes in v2:
time: 488 us; the launch traced here: 486 us
  waiting for transfers between devices  270 us (55%)
  local copies, waits for them, and re-layouts  66.9 us (14%)
  matrix products  58.4 us (12%)
  other arithmetic  34.7 us (7%)
  starting transfers between devices  31.1 us (6%)
  between operations  14.4 us (3%)
  blocking collectives  10.9 us (2%)
    reduce_scatter x3, waiting for transfers between devices, shards(): lax.psum_scatter(part.reshape(local_count, model_width, hidden_count).ast...  130 us
    all_to_all x1, waiting for transfers between devices, shards(): lax.all_to_all(out_send, ('expert', 'seq'), split_axis=0, concat_axis=0,...  68.7 us
    all_to_all x1, waiting for transfers between devices, shards(): lax.all_to_all(in_send, ('expert', 'seq'), split_axis=0, concat_axis=0, t...  68.7 us
    all_to_all x1, blocking collectives, join_halves(): return lax.all_to_all(both, 'core', split_axis=0, concat_axis=0, tiled=True)  10.9 us
    dot_general x1, matrix products, shards(): jnp.einsum('emf,ecdf->ecdm', up_grad, up_h, preferred_element_type=jnp.fl...  10.5 us
    dot_general x1, local copies, waits for them, and re-layouts, shards(): jnp.einsum('cemd,emf->ecdf', in_rows, gate_grad, preferred_element_type=j...  10.2 us
    dot_general x1, local copies, waits for them, and re-layouts, shards(): jnp.einsum('cemd,emf->ecdf', scaled, hidden_low, preferred_element_type=j...  10.1 us
    add x1, local copies, waits for them, and re-layouts, shards(): input_terms + jnp.einsum('emf,ecdf->ecdm', up_grad, up_h, preferred_eleme...  9.95 us
  transfers between devices with their start and end apart: 12, of which 6 were waited for; matrix products, arithmetic and copies ran while one was open for 23% of the time, Pallas kernels for 0%

profile of v2, /device:TPU:0, one launch (start us, length us, event | category | flops | bytes accessed | tf_op | source)
XLA Modules:
  0.0 486.0 jit_solution(3478878139586502497)
XLA Ops:
  13.5 2.9 scatter_custom_fusion
  16.4 3.5 gather_fusion
  20.6 8.1 %all-to-all-start = ((bf16[16,1,32]{2,1,0:T(2,128)(2,1)}), bf16[16,1,32]{2,1,0:T(2,128)(2,1)S(1)}, u32[]{:S(2)}, u32[]{:S(2)}) async-start(bf16[16,1,32]{2,1,0:T(2,128)(2,1)} %all_to_all.28), calls=%async_computation | async-start | bytes 16384 | tf_op jit(solution)/shard_map/all_to_all | solution.py:50
  30.8 4.2 gather_fusion.2
  35.0 4.2 gather_fusion.1
  39.2 6.8 %broadcast_multiply_fusion = (bf16[16,32,3584]{2,1,0:T(8,128)(2,1)}, bf16[16,32,3584]{2,1,0:T(8,128)(2,1)}) fusion(bf16[16,32,3584]{2,1,0:T(8,128)(2,1)} %bitcast.79, bf16[16,32]{1,0:T(8,128)(2,1)S(1)} %reshape.328, bf16[16,32,3584]{2,1,0:T(8,128)(2,1)} %bitcast.80), kind=kLoop, calls=%fused_computation.18 | loop fusion | flops 3670016 | bytes 14681088 | tf_op jit(solution)/shard_map/mul | solution.py:45
  46.0 7.2 %all-to-all-start.3 = ((bf16[16,32,3584]{2,1,0:T(8,128)(2,1)}), bf16[16,32,3584]{2,1,0:T(8,128)(2,1)}, u32[]{:S(2)}, u32[]{:S(2)}) async-start(bf16[16,32,3584]{2,1,0:T(8,128)(2,1)} %get-tuple-element.42), calls=%async_computation.3 | async-start | bytes 7340032 | tf_op jit(solution)/shard_map/all_to_all | solution.py:48
  54.0 68.7 %all-to-all-done.3 = bf16[16,32,3584]{2,1,0:T(8,128)(2,1)} async-done(((bf16[16,32,3584]{2,1,0:T(8,128)(2,1)}), bf16[16,32,3584]{2,1,0:T(8,128)(2,1)}, u32[]{:S(2)}, u32[]{:S(2)}) %all-to-all-start.3) | async-done | bytes 3670048 | tf_op jit(solution)/shard_map/all_to_all | solution.py:48
  122.6 4.5 all-to-all-start.1
  127.3 68.7 %all-to-all-done.1 = bf16[16,32,3584]{2,1,0:T(8,128)(2,1)} async-done(((bf16[16,32,3584]{2,1,0:T(8,128)(2,1)}), bf16[16,32,3584]{2,1,0:T(8,128)(2,1)}, u32[]{:S(2)}, u32[]{:S(2)}) %all-to-all-start.1) | async-done | bytes 3670048 | tf_op jit(solution)/shard_map/all_to_all | solution.py:49
  196.0 2.9 broadcast_in_dim.13
  198.9 10.9 %all_to_all.35 = bf16[2,16,32,3584]{3,2,1,0:T(8,128)(2,1)} all-to-all(bf16[2,16,32,3584]{3,2,1,0:T(8,128)(2,1)S(1)} %broadcast_in_dim.13), channel_id=1, replica_groups=mesh['expert'=4,'seq'=4,'tx'=4,'core'=2] {'core'}, dimensions={0} | all-to-all | bytes 14680064 | tf_op jit(solution)/shard_map/all_to_all | solution.py:55
  209.7 5.8 %broadcast_in_dim.14 = bf16[2,16,32,3584]{3,2,1,0:T(8,128)(2,1)} broadcast(bf16[16,32,3584]{2,1,0:T(8,128)(2,1)} %all-to-all-done.3), dimensions={1,2,3} | broadcast | bytes 11010048 | tf_op jit(solution)/shard_map/broadcast_in_dim | solution.py:54
  215.6 6.6 %all-to-all-start.4 = ((bf16[2,16,32,3584]{3,2,1,0:T(8,128)(2,1)}), bf16[2,16,32,3584]{3,2,1,0:T(8,128)(2,1)}, u32[]{:S(2)}, u32[]{:S(2)}) async-start(bf16[2,16,32,3584]{3,2,1,0:T(8,128)(2,1)} %broadcast_in_dim.14), calls=%async_computation.4 | async-start | bytes 14680064 | tf_op jit(solution)/shard_map/all_to_all | solution.py:55
  222.4 6.2 %convolution_bitcast_fusion.2 = f32[512,256]{0,1:T(8,128)S(1)} fusion(bf16[2,512,3584]{2,1,0:T(8,128)(2,1)} %bitcast.77, bf16[2,3584,256]{2,1,0:T(8,128)(2,1)} %bitcast.88), kind=kOutput, calls=%fused_computation.22 | convolution fusion | flops 1879048192 | bytes 11534336 | tf_op jit(solution)/shard_map/cemd,ecdf->emf/dot_general | solution.py:85
  228.9 6.2 %convolution_bitcast_fusion.1 = f32[512,256]{0,1:T(8,128)S(1)} fusion(bf16[2,512,3584]{2,1,0:T(8,128)(2,1)} %bitcast.6, bf16[2,3584,256]{2,1,0:T(8,128)(2,1)} %bitcast.82), kind=kOutput, calls=%fused_computation.21 | convolution fusion | flops 1879048192 | bytes 11534336 | tf_op jit(solution)/shard_map/cemd,ecdf->emf/dot_general | solution.py:80
  235.2 6.6 %multiply_convert_fusion.2 = (bf16[512,256]{0,1:T(8,128)(2,1)S(1)}, bf16[512]{0:T(512)(128)(2,1)S(1)}, bf16[512,256]{0,1:T(8,128)(2,1)S(1)}, f32[512,256]{0,1:T(8,128)S(1)}) fusion(f32[512,256]{0,1:T(8,128)S(1)} %convolution_bitcast_fusion.1, f32[512,256]{0,1:T(8,128)S(1)} %convolution_bitcast_fusion.2, f32[512]{0:T(512)S(1)} %reshape.327, ...), kind=kOutput, calls=%fused_computation.26 | convolution fusion | flops 1881275904 | bytes 13110272 | tf_op jit(solution)/shard_map/cemd,ecdf->emf/dot_general | solution.py:79
  241.8 7.3 %fusion.9 = f32[512,2,3584]{2,0,1:T(8,128)} fusion(bf16[2,3584,256]{2,1,0:T(8,128)(2,1)S(1)} %bitcast.85, bf16[512,256]{0,1:T(8,128)(2,1)S(1)} %get-tuple-element.39), kind=kOutput, calls=%fused_computation.30 | convolution fusion | flops 1879048192 | bytes 18612224 | tf_op jit(solution)/shard_map/emf,ecdf->ecdm/dot_general | solution.py:93
  249.1 10.5 %fusion.6 = bf16[2,3584,512]{1,2,0:T(8,128)(2,1)} fusion(f32[512,2,3584]{2,0,1:T(8,128)} %fusion.9, bf16[2,3584,256]{2,1,0:T(8,128)(2,1)S(1)} %bitcast.83, bf16[512,256]{0,1:T(8,128)(2,1)S(1)} %get-tuple-element.41), kind=kOutput, calls=%fused_computation.17 | convolution fusion | flops 1886388224 | bytes 25952256 | tf_op jit(solution)/shard_map/emf,ecdf->ecdm/dot_general | solution.py:96
  259.6 10.0 %copy.55 = bf16[2,3584,512]{2,1,0:T(8,128)(2,1)} copy(bf16[2,3584,512]{1,2,0:T(8,128)(2,1)} %fusion.6) | data formatting | bytes 14680064 | tf_op jit(solution)/shard_map/add | solution.py:96
  269.6 6.9 %fusion.4 = bf16[8,912,512]{2,1,0:T(8,128)(2,1)} fusion(bf16[8,1,512]{2,1,0:T(2,128)(2,1)S(1)} %broadcast.252, bf16[8,896,512]{2,1,0:T(8,128)(2,1)} %bitcast.78), kind=kLoop, calls=%fused_computation.15 | loop fusion | flops 22413312 | bytes 14819328 | tf_op jit(solution)/shard_map/concatenate | solution.py:106
  276.7 8.3 %fusion.5 = bf16[2,3584,512]{1,2,0:T(8,128)(2,1)} fusion(f32[512]{0:T(512)S(1)} %reshape.327, bf16[2,16,32,3584]{3,2,1,0:T(8,128)(2,1)} %all_to_all.35), kind=kLoop, calls=%fused_computation.16 | loop fusion | flops 11010048 | bytes 14682112 | tf_op jit(solution)/shard_map/cemd,emf->ecdf/dot_general | solution.py:125
  285.0 10.1 %copy.58 = bf16[2,3584,512]{2,1,0:T(8,128)(2,1)} copy(bf16[2,3584,512]{1,2,0:T(8,128)(2,1)} %fusion.5) | data formatting | bytes 14680064 | tf_op jit(solution)/shard_map/cemd,emf->ecdf/dot_general | solution.py:125
  295.1 7.2 %fusion.3 = bf16[1,7168,256]{2,1,0:T(8,128)(2,1)} fusion(bf16[7168,512]{1,0:T(8,128)(2,1)} %bitcast.81, f32[512,256]{0,1:T(8,128)S(1)} %convolution_bitcast_fusion.1, f32[512,256]{0,1:T(8,128)S(1)} %get-tuple-element.46), kind=kOutput, calls=%fused_computation.14 | convolution fusion | flops 1881669632 | bytes 12058624 | tf_op jit(solution)/shard_map/cemd,emf->ecdf/dot_general | solution.py:125
  302.4 10.2 %copy.57 = bf16[2,3584,512]{2,1,0:T(8,128)(2,1)} copy(bf16[2,3584,512]{1,2,0:T(8,128)(2,1)} %bitcast.19) | data formatting | bytes 14680064 | tf_op jit(solution)/shard_map/cemd,emf->ecdf/dot_general | solution.py:123
  312.5 7.2 %fusion.2 = bf16[1,7168,256]{2,1,0:T(8,128)(2,1)} fusion(bf16[7168,512]{1,0:T(8,128)(2,1)} %bitcast.74, bf16[512,256]{0,1:T(8,128)(2,1)S(1)} %get-tuple-element.41), kind=kOutput, calls=%fused_computation.13 | convolution fusion | flops 1880883200 | bytes 11272192 | tf_op jit(solution)/shard_map/cemd,emf->ecdf/dot_general | solution.py:124
  319.8 7.1 %fusion.1 = bf16[1,7168,256]{2,1,0:T(8,128)(2,1)} fusion(bf16[7168,512]{1,0:T(8,128)(2,1)} %bitcast.75, bf16[512,256]{0,1:T(8,128)(2,1)S(1)} %get-tuple-element.39), kind=kOutput, calls=%fused_computation.12 | convolution fusion | flops 1880883200 | bytes 11272192 | tf_op jit(solution)/shard_map/cemd,emf->ecdf/dot_general | solution.py:123
  329.2 3.9 all-to-all-start.5
  333.2 45.5 %reduce-scatter.11.cloned.1.call-done = bf16[1,1792,256]{2,1,0:T(8,128)(2,1)} async-done(((bf16[1,7168,256]{2,1,0:T(8,128)(2,1)}), bf16[1,1792,256]{2,1,0:T(8,128)(2,1)}) %reduce-scatter.11.cloned.1.call-update) | async-done | bytes 917520 | tf_op jit(solution)/shard_map/reduce_scatter | solution.py:127
  378.7 2.5 convert_element_type.105
  381.2 42.1 %reduce-scatter.9.cloned.1.call-done = bf16[1,1792,256]{2,1,0:T(8,128)(2,1)} async-done(((bf16[1,7168,256]{2,1,0:T(8,128)(2,1)}), bf16[1,1792,256]{2,1,0:T(8,128)(2,1)}) %reduce-scatter.9.cloned.1.call-update) | async-done | bytes 917520 | tf_op jit(solution)/shard_map/reduce_scatter | solution.py:127
  425.9 42.3 %reduce-scatter.7.cloned.1.call-done = bf16[1,1792,256]{2,1,0:T(8,128)(2,1)} async-done(((bf16[1,7168,256]{2,1,0:T(8,128)(2,1)}), bf16[1,1792,256]{2,1,0:T(8,128)(2,1)}) %reduce-scatter.7.cloned.1.call-update) | async-done | bytes 917520 | tf_op jit(solution)/shard_map/reduce_scatter | solution.py:127
  (64 shorter events, 26.5 us)
Async XLA Ops:
  7.2 215.3 %all-gather.4.cloned.1.call-start = ((), (), s32[]{:S(2)}) async-start(), calls=%async_computation.10 | async-start | bytes 4587520 | tf_op jit(solution)/shard_map/all_gather | solution.py:73
  7.9 221.0 %all-gather.6.cloned.1.call-start = ((), (), s32[]{:S(2)}) async-start(), calls=%async_computation.11 | async-start | bytes 4587520 | tf_op jit(solution)/shard_map/all_gather | solution.py:72
  20.6 25.4 %all-to-all-start = ((bf16[16,1,32]{2,1,0:T(2,128)(2,1)}), bf16[16,1,32]{2,1,0:T(2,128)(2,1)S(1)}, u32[]{:S(2)}, u32[]{:S(2)}) async-start(bf16[16,1,32]{2,1,0:T(2,128)(2,1)} %all_to_all.28), calls=%async_computation | async-start | bytes 16384 | tf_op jit(solution)/shard_map/all_to_all | solution.py:50
  46.0 76.6 %all-to-all-start.3 = ((bf16[16,32,3584]{2,1,0:T(8,128)(2,1)}), bf16[16,32,3584]{2,1,0:T(8,128)(2,1)}, u32[]{:S(2)}, u32[]{:S(2)}) async-start(bf16[16,32,3584]{2,1,0:T(8,128)(2,1)} %get-tuple-element.42), calls=%async_computation.3 | async-start | bytes 7340032 | tf_op jit(solution)/shard_map/all_to_all | solution.py:48
  53.2 181.9 %all-gather.8.cloned.1.call-start = ((), (), s32[]{:S(2)}) async-start(), calls=%async_computation.12 | async-start | bytes 4587520 | tf_op jit(solution)/shard_map/all_gather | solution.py:71
  122.6 73.3 %all-to-all-start.1 = ((bf16[16,32,3584]{2,1,0:T(8,128)(2,1)}), bf16[16,32,3584]{2,1,0:T(8,128)(2,1)}, u32[]{:S(2)}, u32[]{:S(2)}) async-start(bf16[16,32,3584]{2,1,0:T(8,128)(2,1)} %get-tuple-element.43), calls=%async_computation.1 | async-start | bytes 7340032 | tf_op jit(solution)/shard_map/all_to_all | solution.py:49
  215.6 13.3 %all-to-all-start.4 = ((bf16[2,16,32,3584]{3,2,1,0:T(8,128)(2,1)}), bf16[2,16,32,3584]{3,2,1,0:T(8,128)(2,1)}, u32[]{:S(2)}, u32[]{:S(2)}) async-start(bf16[2,16,32,3584]{3,2,1,0:T(8,128)(2,1)} %broadcast_in_dim.14), calls=%async_computation.4 | async-start | bytes 14680064 | tf_op jit(solution)/shard_map/all_to_all | solution.py:55
  222.2 104.8 %reduce-scatter.5.cloned.1.call-start = ((), (), s32[]{:S(2)}) async-start(), calls=%async_computation.13 | async-start | bytes 8404992 | tf_op jit(solution)/shard_map/reduce_scatter | solution.py:107
  235.2 6.7 %copy-start.1 = (bf16[1,7168,256]{2,1,0:T(8,128)(2,1)S(1)}, bf16[1,7168,256]{2,1,0:T(8,128)(2,1)}, u32[]{:S(2)}) copy-start(bf16[1,7168,256]{2,1,0:T(8,128)(2,1)} %all-gather.8.cloned.1.call-done) | copy-start | bytes 11010052
  241.8 7.3 %copy-start = (bf16[1,7168,256]{2,1,0:T(8,128)(2,1)S(1)}, bf16[1,7168,256]{2,1,0:T(8,128)(2,1)}, u32[]{:S(2)}) copy-start(bf16[1,7168,256]{2,1,0:T(8,128)(2,1)} %all-gather.6.cloned.1.call-done) | copy-start | bytes 11010052
  276.5 102.2 %reduce-scatter.11.cloned.1.call-start = ((), (), s32[]{:S(2)}) async-start(), calls=%async_computation.16 | async-start | bytes 4587520 | tf_op jit(solution)/shard_map/reduce_scatter | solution.py:127
  302.3 121.0 %reduce-scatter.9.cloned.1.call-start = ((), (), s32[]{:S(2)}) async-start(), calls=%async_computation.15 | async-start | bytes 4587520 | tf_op jit(solution)/shard_map/reduce_scatter | solution.py:127
  319.7 148.5 %reduce-scatter.7.cloned.1.call-start = ((), (), s32[]{:S(2)}) async-start(), calls=%async_computation.14 | async-start | bytes 4587520 | tf_op jit(solution)/shard_map/reduce_scatter | solution.py:127
  329.2 141.5 %all-to-all-start.5 = ((bf16[16,32,912]{2,1,0:T(8,128)(2,1)}), bf16[16,32,912]{2,1,0:T(8,128)(2,1)S(1)}, u32[]{:S(2)}, u32[]{:S(2)}) async-start(bf16[16,32,912]{2,1,0:T(8,128)(2,1)} %bitcast.17), calls=%async_computation.6 | async-start | bytes 2097152 | tf_op jit(solution)/shard_map/all_to_all | solution.py:116
  473.6 1.4 slice-start
Sparse Core Ops, SparseCore 0:
  9.7 46.4 all-gather.3
  57.8 67.4 all-gather.5
  127.0 67.6 all-gather.7
  276.6 46.2 reduce-scatter.4
  325.2 53.4 reduce-scatter.10
  381.1 42.2 reduce-scatter.8
  425.9 42.2 reduce-scatter.6
